TPU v7x, 32 devices: a whole 2x2x4 slice. The times are simulated.
32 devices in a mesh: dp: 2 (over core), row: 4 (over y, x), col: 4 (over z).
Axes of the slice: x: 2, y: 2, z: 4, core: 2. Of those that a mesh axis runs over, the one named last changes fastest.
Arguments:
- block_input: bfloat16 [8192, 2048], P(('dp', 'row')), may hold values from -6 to 6
- segment_ids: int32 [8192], P(('dp', 'row')), may hold values from 0 to 3, as said below
- positions: int32 [8192], P(('dp', 'row')), may hold values from 0 to 1023, as said below
- w_query: bfloat16 [2048, 2048], P('row', 'col'), as said below
- w_key: bfloat16 [2048, 2048], P('row', 'col'), as said below
- w_value: bfloat16 [2048, 2048], P('row', 'col'), may hold values from -0.125 to 0.125
- w_out: bfloat16 [2048, 2048], P('col', 'row'), may hold values from -0.125 to 0.125
- w_gate: bfloat16 [2048, 8192], P('row', 'col'), may hold values from -0.125 to 0.125
- w_up: bfloat16 [2048, 8192], P('row', 'col'), may hold values from -0.125 to 0.125
- w_down: bfloat16 [8192, 2048], P('col', 'row'), may hold values from -0.0625 to 0.0625
- query_gain: float32 [2048], P('col'), may hold values from 0.25 to 1.75
- key_gain: float32 [2048], P('col'), may hold values from 0.25 to 1.75
- attn_gain: float32 [2048], replicated, may hold values from 0.25 to 1.75
- mlp_gain: float32 [2048], replicated, may hold values from 0.25 to 1.75
- grad_output: bfloat16 [8192, 2048], P(('dp', 'row')), as said below
Outputs:
- block_output: bfloat16 [8192, 2048], P(('dp', 'row'))
- grad_input: float32 [8192, 2048], P(('dp', 'row'))
- grad_w_query: float32 [2048, 2048], P('row', 'col')
- grad_w_key: float32 [2048, 2048], P('row', 'col')
- grad_w_value: float32 [2048, 2048], P('row', 'col')
- grad_w_out: float32 [2048, 2048], P('col', 'row')
- grad_w_gate: float32 [2048, 8192], P('row', 'col')
- grad_w_up: float32 [2048, 8192], P('row', 'col')
- grad_w_down: float32 [8192, 2048], P('col', 'row')
- grad_query_gain: float32 [2048], P('col')
- grad_key_gain: float32 [2048], P('col')
- grad_attn_gain: float32 [2048], replicated
- grad_mlp_gain: float32 [2048], replicated
Inputs may be any that keep to these rules, and one draw needn't show every extreme that they name: `segment_ids`: within each sequence of 1024 tokens the ids never fall. `positions`: the index of a token counted from the first token with the same id in its sequence. `w_query`: scaled to the fan-in 2048. `w_key`: scaled to the fan-in 2048. `grad_output`: of order one in every row.
All inputs are finite; a program needn't handle non-finite values.
Results may differ from a plain program's by a relative error of at most 0.02.
Values may be sent and summed in bfloat16 or wider, within the bound.
No kernel may reach another device: no remote copies, remote signals or barrier semaphores. Data moves between devices by JAX's collectives and lax.ppermute only.
A program may use at most 320 MiB of HBM per device.

v0:
```python
import jax
import jax.numpy as jnp
from jax import lax
from jax.sharding import PartitionSpec as P

HD = 128
LEN = 1024
EPS = 1e-06
THETA = 500000.0
NEG_FILL = -1e30


def plain_dot(left_mat, right_mat):
    return jnp.dot(left_mat, right_mat, preferred_element_type=jnp.float32)


def times_transposed(left_mat, right_mat):
    return lax.dot_general(
        left_mat, right_mat, (((1,), (1,)), ((), ())), preferred_element_type=jnp.float32
    )


def left_transposed(left_mat, right_mat):
    return lax.dot_general(
        left_mat, right_mat, (((0,), (0,)), ((), ())), preferred_element_type=jnp.float32
    )


def rope_tables(positions):
    half_dim = HD // 2
    inv_freq = THETA ** (-(jnp.arange(half_dim, dtype=jnp.float32) * 2.0) / HD)
    angles = positions.astype(jnp.float32)[:, None] * inv_freq[None, :]
    cosine = jnp.concatenate([jnp.cos(angles), jnp.cos(angles)], axis=-1)
    sine_tab = jnp.concatenate([jnp.sin(angles), jnp.sin(angles)], axis=-1)
    return (cosine, sine_tab)


def rotate(values):
    first_half = values[..., : HD // 2]
    second_half = values[..., HD // 2 :]
    return jnp.concatenate([-second_half, first_half], axis=-1)


def rotate_back(values):
    first_half = values[..., : HD // 2]
    second_half = values[..., HD // 2 :]
    return jnp.concatenate([second_half, -first_half], axis=-1)


def block_mask(seg_seq, first_row, block_rows):
    length = seg_seq.shape[0]
    query_index = first_row + jnp.arange(block_rows)
    key_index = jnp.arange(length)
    query_seg = seg_seq[first_row : first_row + block_rows]
    return (
        (query_seg[:, None] == seg_seq[None, :]) & (key_index[None, :] <= query_index[:, None])
    )[None]


def attend_forward(packed):
    query_rot, key_rot, value_heads, seg_seq = packed
    length = query_rot.shape[0]
    block_rows = min(512, length)
    score_scale = HD ** (-0.5)
    output_list = []
    log_list = []
    for first_row in range(0, length, block_rows):
        query_blk = query_rot[first_row : first_row + block_rows]
        scores = (
            jnp.einsum("qhd,khd->hqk", query_blk, key_rot, preferred_element_type=jnp.float32)
            * score_scale
        )
        allowed = block_mask(seg_seq, first_row, block_rows)
        masked = jnp.where(allowed, scores, NEG_FILL)
        row_peak = jnp.max(masked, axis=-1, keepdims=True)
        row_total = jnp.sum(jnp.exp(masked - row_peak), axis=-1, keepdims=True)
        log_total = row_peak + jnp.log(row_total)
        probs_b = jnp.where(allowed, jnp.exp(scores - log_total), 0.0).astype(jnp.bfloat16)
        attended = jnp.einsum(
            "hqk,khd->qhd", probs_b, value_heads, preferred_element_type=jnp.float32
        ).astype(jnp.bfloat16)
        output_list.append(attended)
        log_list.append(log_total[..., 0])
    return (jnp.concatenate(output_list, axis=0), jnp.concatenate(log_list, axis=1))


def attend_backward(packed):
    query_rot, key_rot, value_heads, seg_seq, attended, log_total, grad_att = packed
    length = query_rot.shape[0]
    block_rows = min(512, length)
    score_scale = HD ** (-0.5)
    delta = jnp.sum(grad_att.astype(jnp.float32) * attended.astype(jnp.float32), axis=-1)
    grad_key = jnp.zeros(key_rot.shape, jnp.float32)
    grad_value = jnp.zeros(value_heads.shape, jnp.float32)
    grad_query_list = []
    for first_row in range(0, length, block_rows):
        query_blk = query_rot[first_row : first_row + block_rows]
        grad_blk = grad_att[first_row : first_row + block_rows]
        scores = (
            jnp.einsum("qhd,khd->hqk", query_blk, key_rot, preferred_element_type=jnp.float32)
            * score_scale
        )
        allowed = block_mask(seg_seq, first_row, block_rows)
        probs = jnp.where(
            allowed, jnp.exp(scores - log_total[:, first_row : first_row + block_rows, None]), 0.0
        )
        probs_b = probs.astype(jnp.bfloat16)
        grad_probs = jnp.einsum(
            "qhd,khd->hqk", grad_blk, value_heads, preferred_element_type=jnp.float32
        )
        delta_blk = jnp.transpose(delta[first_row : first_row + block_rows])[:, :, None]
        grad_scores = (probs * (grad_probs - delta_blk) * score_scale).astype(jnp.bfloat16)
        grad_query_list.append(
            jnp.einsum("hqk,khd->qhd", grad_scores, key_rot, preferred_element_type=jnp.float32)
        )
        grad_key = grad_key + jnp.einsum(
            "hqk,qhd->khd", grad_scores, query_blk, preferred_element_type=jnp.float32
        )
        grad_value = grad_value + jnp.einsum(
            "hqk,qhd->khd", probs_b, grad_blk, preferred_element_type=jnp.float32
        )
    return (jnp.concatenate(grad_query_list, axis=0), grad_key, grad_value)


def shards(
    block_input,
    segment_ids,
    positions,
    w_query,
    w_key,
    w_value,
    w_out,
    w_gate,
    w_up,
    w_down,
    query_gain,
    key_gain,
    attn_gain,
    mlp_gain,
    grad_output,
):
    tokens_here = block_input.shape[0]
    seq_count = tokens_here // LEN
    width = block_input.shape[1]
    local_width = w_query.shape[1]
    local_heads = local_width // HD
    gathered = (
        lax.all_gather(w_query, "row", axis=0, tiled=True),
        lax.all_gather(w_key, "row", axis=0, tiled=True),
        lax.all_gather(w_value, "row", axis=0, tiled=True),
        lax.all_gather(w_out, "row", axis=1, tiled=True),
        lax.all_gather(w_gate, "row", axis=0, tiled=True),
        lax.all_gather(w_up, "row", axis=0, tiled=True),
        lax.all_gather(w_down, "row", axis=1, tiled=True),
    )
    full_query, full_key, full_value, full_out, full_gate, full_up, full_down = gathered
    query_raw = plain_dot(block_input, full_query)
    key_raw = plain_dot(block_input, full_key)
    value_raw = plain_dot(block_input, full_value)
    query_sq, key_sq = lax.psum(
        (jnp.sum(query_raw * query_raw, axis=1), jnp.sum(key_raw * key_raw, axis=1)), "col"
    )
    query_scale = lax.rsqrt(query_sq / width + EPS)[:, None]
    key_scale = lax.rsqrt(key_sq / width + EPS)[:, None]
    query_unit = query_raw * query_scale
    key_unit = key_raw * key_scale
    cosine, sine_tab = rope_tables(positions)

    def turn(values):
        head_view = values.reshape(tokens_here, local_heads, HD)
        return head_view * cosine[:, None, :] + rotate(head_view) * sine_tab[:, None, :]

    def unturn(values):
        back = values * cosine[:, None, :] + rotate_back(values * sine_tab[:, None, :])
        return back.reshape(tokens_here, local_width)

    seq_shape = (seq_count, LEN, local_heads, HD)
    query_rot = turn(query_unit * query_gain).astype(jnp.bfloat16).reshape(seq_shape)
    key_rot = turn(key_unit * key_gain).astype(jnp.bfloat16).reshape(seq_shape)
    value_heads = value_raw.astype(jnp.bfloat16).reshape(seq_shape)
    seg_view = segment_ids.reshape(seq_count, LEN)
    attended, log_total = lax.map(attend_forward, (query_rot, key_rot, value_heads, seg_view))
    attended_flat = attended.reshape(tokens_here, local_width)
    attn_raw = lax.psum(plain_dot(attended_flat, full_out), "col")
    attn_scale = lax.rsqrt(jnp.mean(attn_raw * attn_raw, axis=1, keepdims=True) + EPS)
    attn_unit = attn_raw * attn_scale
    hidden = block_input.astype(jnp.float32) + attn_unit * attn_gain
    hidden_b = hidden.astype(jnp.bfloat16)
    gate_proj = plain_dot(hidden_b, full_gate)
    up_proj = plain_dot(hidden_b, full_up)
    gate_sig = jax.nn.sigmoid(gate_proj)
    gate_act = gate_proj * gate_sig
    mixed_act = (gate_act * up_proj).astype(jnp.bfloat16)
    down_raw = lax.psum(plain_dot(mixed_act, full_down), "col")
    down_scale = lax.rsqrt(jnp.mean(down_raw * down_raw, axis=1, keepdims=True) + EPS)
    down_unit = down_raw * down_scale
    block_output = (hidden + down_unit * mlp_gain).astype(jnp.bfloat16)
    regathered = (
        lax.all_gather(w_query, "row", axis=0, tiled=True),
        lax.all_gather(w_key, "row", axis=0, tiled=True),
        lax.all_gather(w_value, "row", axis=0, tiled=True),
        lax.all_gather(w_out, "row", axis=1, tiled=True),
        lax.all_gather(w_gate, "row", axis=0, tiled=True),
        lax.all_gather(w_up, "row", axis=0, tiled=True),
        lax.all_gather(w_down, "row", axis=1, tiled=True),
    )
    full_query, full_key, full_value, full_out, full_gate, full_up, full_down = regathered
    grad_y = grad_output.astype(jnp.float32)
    grad_mlp_gain = jnp.sum(grad_y * down_unit, axis=0)
    down_dz = grad_y * mlp_gain
    grad_down_in = (
        down_scale * (down_dz - down_unit * jnp.mean(down_dz * down_unit, axis=1, keepdims=True))
    ).astype(jnp.bfloat16)
    grad_w_down = left_transposed(mixed_act, grad_down_in)
    grad_mixed = times_transposed(grad_down_in, full_down)
    grad_gate_in = (grad_mixed * up_proj * gate_sig * (1.0 + gate_proj * (1.0 - gate_sig))).astype(
        jnp.bfloat16
    )
    grad_up_in = (grad_mixed * gate_act).astype(jnp.bfloat16)
    grad_w_gate = left_transposed(hidden_b, grad_gate_in)
    grad_w_up = left_transposed(hidden_b, grad_up_in)
    mlp_part = times_transposed(grad_gate_in, full_gate) + times_transposed(grad_up_in, full_up)
    grad_hidden = grad_y + lax.psum(mlp_part, "col")
    grad_attn_gain = jnp.sum(grad_hidden * attn_unit, axis=0)
    attn_dz = grad_hidden * attn_gain
    grad_attn_in = (
        attn_scale * (attn_dz - attn_unit * jnp.mean(attn_dz * attn_unit, axis=1, keepdims=True))
    ).astype(jnp.bfloat16)
    grad_w_out = left_transposed(attended_flat, grad_attn_in)
    grad_att = times_transposed(grad_attn_in, full_out).astype(jnp.bfloat16).reshape(seq_shape)
    grad_query_rot, grad_key_rot, grad_value_heads = lax.map(
        attend_backward, (query_rot, key_rot, value_heads, seg_view, attended, log_total, grad_att)
    )
    head_shape = (tokens_here, local_heads, HD)
    grad_query_norm = unturn(grad_query_rot.reshape(head_shape))
    grad_key_norm = unturn(grad_key_rot.reshape(head_shape))
    grad_query_gain = jnp.sum(grad_query_norm * query_unit, axis=0)
    grad_key_gain = jnp.sum(grad_key_norm * key_unit, axis=0)
    query_dz = grad_query_norm * query_gain
    key_dz = grad_key_norm * key_gain
    query_dot, key_dot = lax.psum(
        (jnp.sum(query_dz * query_unit, axis=1), jnp.sum(key_dz * key_unit, axis=1)), "col"
    )
    grad_query_in = (query_scale * (query_dz - query_unit * (query_dot / width)[:, None])).astype(
        jnp.bfloat16
    )
    grad_key_in = (key_scale * (key_dz - key_unit * (key_dot / width)[:, None])).astype(
        jnp.bfloat16
    )
    grad_value_in = grad_value_heads.reshape(tokens_here, local_width).astype(jnp.bfloat16)
    input_part = (
        times_transposed(grad_query_in, full_query)
        + times_transposed(grad_key_in, full_key)
        + times_transposed(grad_value_in, full_value)
    )
    grad_input = grad_hidden + lax.psum(input_part.astype(jnp.bfloat16), "col").astype(jnp.float32)
    grad_w_query = left_transposed(block_input, grad_query_in)
    grad_w_key = left_transposed(block_input, grad_key_in)
    grad_w_value = left_transposed(block_input, grad_value_in)
    row_grads = (
        lax.psum_scatter(
            grad_w_query.astype(jnp.bfloat16), "row", scatter_dimension=0, tiled=True
        ).astype(jnp.float32),
        lax.psum_scatter(
            grad_w_key.astype(jnp.bfloat16), "row", scatter_dimension=0, tiled=True
        ).astype(jnp.float32),
        lax.psum_scatter(
            grad_w_value.astype(jnp.bfloat16), "row", scatter_dimension=0, tiled=True
        ).astype(jnp.float32),
        lax.psum_scatter(
            grad_w_out.astype(jnp.bfloat16), "row", scatter_dimension=1, tiled=True
        ).astype(jnp.float32),
        lax.psum_scatter(
            grad_w_gate.astype(jnp.bfloat16), "row", scatter_dimension=0, tiled=True
        ).astype(jnp.float32),
        lax.psum_scatter(
            grad_w_up.astype(jnp.bfloat16), "row", scatter_dimension=0, tiled=True
        ).astype(jnp.float32),
        lax.psum_scatter(
            grad_w_down.astype(jnp.bfloat16), "row", scatter_dimension=1, tiled=True
        ).astype(jnp.float32),
    )
    data_grads = (
        lax.psum(row_grads[0].astype(jnp.bfloat16), "dp").astype(jnp.float32),
        lax.psum(row_grads[1].astype(jnp.bfloat16), "dp").astype(jnp.float32),
        lax.psum(row_grads[2].astype(jnp.bfloat16), "dp").astype(jnp.float32),
        lax.psum(row_grads[3].astype(jnp.bfloat16), "dp").astype(jnp.float32),
        lax.psum(row_grads[4].astype(jnp.bfloat16), "dp").astype(jnp.float32),
        lax.psum(row_grads[5].astype(jnp.bfloat16), "dp").astype(jnp.float32),
        lax.psum(row_grads[6].astype(jnp.bfloat16), "dp").astype(jnp.float32),
    )
    gain_grads = lax.psum(
        (grad_query_gain, grad_key_gain, grad_attn_gain, grad_mlp_gain), ("dp", "row")
    )
    return (
        block_output,
        grad_input,
        data_grads[0],
        data_grads[1],
        data_grads[2],
        data_grads[3],
        data_grads[4],
        data_grads[5],
        data_grads[6],
        gain_grads[0],
        gain_grads[1],
        gain_grads[2],
        gain_grads[3],
    )


def solution(mesh):
    in_specs = (
        P(("dp", "row"), None),
        P(("dp", "row")),
        P(("dp", "row")),
        P("row", "col"),
        P("row", "col"),
        P("row", "col"),
        P("col", "row"),
        P("row", "col"),
        P("row", "col"),
        P("col", "row"),
        P("col"),
        P("col"),
        P(),
        P(),
        P(("dp", "row"), None),
    )
    out_specs = (
        P(("dp", "row"), None),
        P(("dp", "row"), None),
        P("row", "col"),
        P("row", "col"),
        P("row", "col"),
        P("col", "row"),
        P("row", "col"),
        P("row", "col"),
        P("col", "row"),
        P("col"),
        P("col"),
        P(),
        P(),
    )
    return jax.shard_map(shards, mesh=mesh, in_specs=in_specs, out_specs=out_specs, check_vma=False)
```

profile of v0, /device:TPU:0, one launch (start us, length us, event | category | flops | bytes accessed | tf_op | source)
XLA Modules:
  0.0 2085.5 jit_solution(18045758009475935675)
XLA Ops:
  15.1 32.7 %all-gather.12.cloned.1.call-done = bf16[2048,512]{1,0:T(8,128)(2,1)} async-done(((bf16[512,512]{1,0:T(8,128)(2,1)}), bf16[2048,512]{1,0:T(8,128)(2,1)}) %all-gather.12.cloned.1.call-update) | async-done | bytes 2097168 | tf_op jit(solution)/shard_map/all_gather | solution.py:149
  47.8 6.6 multiply_reduce_fusion.7
  54.4 30.5 %all-gather.10.cloned.1.call-done = bf16[2048,512]{1,0:T(8,128)(2,1)} async-done(((bf16[512,512]{1,0:T(8,128)(2,1)}), bf16[2048,512]{1,0:T(8,128)(2,1)}) %all-gather.10.cloned.1.call-update) | async-done | bytes 2097168 | tf_op jit(solution)/shard_map/all_gather | solution.py:148
  84.8 5.2 multiply_reduce_fusion.8
  90.1 12.1 all-reduce.2
  123.6 4.7 exponential_reduce_fusion
  128.5 5.7 convolution_convert_fusion.8
  141.4 17.3 all-gather.14.cloned.1.call-done
  158.6 7.2 fusion.41
  168.0 288.8 %all-reduce.10.cloned.1.call-done = f32[1024,2048]{1,0:T(8,128)} async-done(((f32[1024,2048]{1,0:T(8,128)}), f32[1024,2048]{1,0:T(8,128)}) %all-reduce.10.cloned.1.call-update) | async-done | bytes 8388624 | tf_op jit(solution)/shard_map/psum | solution.py:184
  456.9 4.1 multiply_reduce_fusion.3
  462.7 4.9 fusion.9
  467.6 77.5 %all-gather.16.cloned.1.call-done = bf16[2048,2048]{1,0:T(8,128)(2,1)} async-done(((bf16[512,2048]{1,0:T(8,128)(2,1)}), bf16[2048,2048]{1,0:T(8,128)(2,1)}) %all-gather.16.cloned.1.call-update) | async-done | bytes 8388624 | tf_op jit(solution)/shard_map/all_gather | solution.py:152
  545.1 14.5 fusion.42
  559.6 74.8 %all-gather.18.cloned.1.call-done = bf16[2048,2048]{1,0:T(8,128)(2,1)} async-done(((bf16[512,2048]{1,0:T(8,128)(2,1)}), bf16[2048,2048]{1,0:T(8,128)(2,1)}) %all-gather.18.cloned.1.call-update) | async-done | bytes 8388624 | tf_op jit(solution)/shard_map/all_gather | solution.py:153
  634.4 17.0 multiply_convert_fusion.5
  651.4 72.3 %all-gather.20.cloned.1.call-done = bf16[2048,2048]{1,0:T(8,128)(2,1)} async-done(((bf16[2048,512]{1,0:T(8,128)(2,1)}), bf16[2048,2048]{1,0:T(8,128)(2,1)}) %all-gather.20.cloned.1.call-update) | async-done | bytes 8388624 | tf_op jit(solution)/shard_map/all_gather | solution.py:154
  723.6 14.5 fusion.43
  738.2 290.9 %all-reduce.12.cloned.1.call-done = f32[1024,2048]{1,0:T(8,128)} async-done(((f32[1024,2048]{1,0:T(8,128)}), f32[1024,2048]{1,0:T(8,128)}) %all-reduce.12.cloned.1.call-update) | async-done | bytes 8388624 | tf_op jit(solution)/shard_map/psum | solution.py:194
  1029.2 4.1 multiply_reduce_fusion.2
  1034.9 5.3 fusion.5
  1042.5 19.7 multiply_convert_fusion.3
  1062.2 12.7 fusion.44
  1074.9 13.6 convolution_add_fusion
  1090.6 287.9 %all-reduce.14.cloned.1.call-done = f32[1024,2048]{1,0:T(8,128)} async-done(((f32[1024,2048]{1,0:T(8,128)}), f32[1024,2048]{1,0:T(8,128)}) %all-reduce.14.cloned.1.call-update) | async-done | bytes 8388624 | tf_op jit(solution)/shard_map/psum | solution.py:223
  1378.5 10.6 multiply_reduce_fusion
  1389.2 13.4 multiply_convert_fusion.2
  1402.6 5.3 fusion.18
  1408.1 5.0 fusion.33
  1413.2 7.3 multiply_convert_fusion.1
  1420.5 5.1 multiply_convert_fusion
  1439.4 4.5 convolution_bitcast_fusion
  1464.6 4.3 multiply_reduce_fusion.4
  1469.6 9.6 all-reduce.1
  1486.4 6.2 convolution_convert_fusion.3
  1499.6 14.4 convolution_convert_fusion
  1514.1 14.1 convolution_convert_fusion.2
  1528.3 14.7 convolution_convert_fusion.1
  1549.4 5.8 add_convert_fusion
  1558.5 38.0 %reduce-scatter.8.cloned.1.call-done = bf16[512,512]{0,1:T(8,128)(2,1)} async-done(((bf16[2048,512]{0,1:T(8,128)(2,1)}), bf16[512,512]{0,1:T(8,128)(2,1)}) %reduce-scatter.8.cloned.1.call-update) | async-done | bytes 524304 | tf_op jit(solution)/shard_map/reduce_scatter | solution.py:261
  1596.5 89.3 %reduce-scatter.20.cloned.1.call-done = bf16[2048,512]{1,0:T(8,128)(2,1)} async-done(((bf16[2048,2048]{1,0:T(8,128)(2,1)}), bf16[2048,512]{1,0:T(8,128)(2,1)}) %reduce-scatter.20.cloned.1.call-update) | async-done | bytes 2097168 | tf_op jit(solution)/shard_map/reduce_scatter | solution.py:279
  1685.8 89.8 %reduce-scatter.16.cloned.1.call-done = bf16[512,2048]{1,0:T(8,128)(2,1)} async-done(((bf16[2048,2048]{1,0:T(8,128)(2,1)}), bf16[512,2048]{1,0:T(8,128)(2,1)}) %reduce-scatter.16.cloned.1.call-update) | async-done | bytes 2097168 | tf_op jit(solution)/shard_map/reduce_scatter | solution.py:273
  1775.6 89.3 %reduce-scatter.18.cloned.1.call-done = bf16[512,2048]{1,0:T(8,128)(2,1)} async-done(((bf16[2048,2048]{1,0:T(8,128)(2,1)}), bf16[512,2048]{1,0:T(8,128)(2,1)}) %reduce-scatter.18.cloned.1.call-update) | async-done | bytes 2097168 | tf_op jit(solution)/shard_map/reduce_scatter | solution.py:276
  1865.6 27.9 %all-reduce = (f32[512]{0:T(512)}, f32[512]{0:T(512)}, f32[2048]{0:T(1024)}, f32[2048]{0:T(1024)}) all-reduce(f32[512]{0:T(512)S(1)} %get-tuple-element.86, f32[512]{0:T(512)S(1)} %get-tuple-element.84, f32[2048]{0:T(1024)S(1)} %copy-done.64, f32[2048]{0:T(1024)S(1)} %copy-done.65), channel_id=1, replica_groups=mesh['dp'=2,'row'=4,'col'=4] {'dp','row'}, use_global_device_ids=true, to_apply=%region_36.37 | all-reduce | flops 5120 | bytes 40960 | tf_op jit(solution)/shard_map/psum | solution.py:292
  1893.5 129.3 %all-reduce.16.cloned.1.call-done = bf16[1024,2048]{1,0:T(8,128)(2,1)} async-done(((bf16[1024,2048]{1,0:T(8,128)(2,1)}), bf16[1024,2048]{1,0:T(8,128)(2,1)}) %all-reduce.16.cloned.1.call-update) | async-done | bytes 4194320 | tf_op jit(solution)/shard_map/psum | solution.py:256
  2022.7 12.0 convert_add_fusion.1
  2034.7 29.7 %all-reduce.18.cloned.1.call-done = (bf16[512,512]{0,1:T(8,128)(2,1)}, bf16[512,512]{0,1:T(8,128)(2,1)}, bf16[512,512]{0,1:T(8,128)(2,1)}, bf16[512,512]{1,0:T(8...) async-done(((bf16[512,512]{0,1:T(8,128)(2,1)}, bf16[512,512]{0,1:T(8,128)(2,1)}, bf16[512,512]{0,1:T(8,128)(2,1)}, ...) | async-done | bytes 8388624 | tf_op jit(solution)/shard_map/psum | solution.py:284
  2064.4 4.3 convert_element_type.217
  (267 shorter events, 115.2 us)
Async XLA Ops:
  7.2 5.9 copy-start.70
  7.2 40.6 %all-gather.12.cloned.1.call-start = ((), (), s32[]{:S(2)}) async-start(), calls=%async_computation.9 | async-start | bytes 2621440 | tf_op jit(solution)/shard_map/all_gather | solution.py:149
  7.9 76.9 %all-gather.10.cloned.1.call-start = ((), (), s32[]{:S(2)}) async-start(), calls=%async_computation.8 | async-start | bytes 2621440 | tf_op jit(solution)/shard_map/all_gather | solution.py:148
  8.7 119.8 %all-gather.8.cloned.1.call-start = ((), (), s32[]{:S(2)}) async-start(), calls=%async_computation.7 | async-start | bytes 2621440 | tf_op jit(solution)/shard_map/all_gather | solution.py:150
  9.4 149.2 %all-gather.14.cloned.1.call-start = ((), (), s32[]{:S(2)}) async-start(), calls=%async_computation.10 | async-start | bytes 2621440 | tf_op jit(solution)/shard_map/all_gather | solution.py:151
  10.0 446.9 %all-reduce.10.cloned.1.call-start = ((), (), s32[]{:S(2)}) async-start(), calls=%async_computation.11 | async-start | bytes 16777216 | tf_op jit(solution)/shard_map/psum | solution.py:184
  12.8 103.1 %copy-start.22 = (f32[1024,128]{1,0:T(8,128)}, f32[1024,128]{1,0:T(8,128)S(1)}, u32[]{:S(2)}) copy-start(f32[1024,128]{1,0:T(8,128)S(1)} %pad_maximum_fusion.2) | copy-start | bytes 1572868
  13.1 102.9 %copy-start.27 = (f32[1024,128]{1,0:T(8,128)}, f32[1024,128]{1,0:T(8,128)S(1)}, u32[]{:S(2)}) copy-start(f32[1024,128]{1,0:T(8,128)S(1)} %pad_maximum_fusion.3) | copy-start | bytes 1572868
  54.3 47.9 %copy-start.68 = (f32[512]{0:T(512)S(1)}, f32[512]{0:T(512)}, u32[]{:S(2)}) copy-start(f32[512]{0:T(512)} %param.25) | copy-start | bytes 6148
  90.1 13.7 copy-start.9
  122.2 6.2 copy-start.5
  128.4 5.8 copy-start.73
  128.4 8.8 copy-start.71
  128.4 5.8 copy-start.32
  128.5 5.9 copy-start.8
  141.4 24.5 %copy-start.46 = (bf16[1024,4,128]{0,2,1:T(8,128)(2,1)}, bf16[1024,4,128]{0,2,1:T(8,128)(2,1)S(1)}, u32[]{:S(2)}) copy-start(bf16[1024,4,128]{0,2,1:T(8,128)(2,1)S(1)} %pad_maximum_fusion.1) | copy-start | bytes 3145732
  165.9 379.2 %all-gather.16.cloned.1.call-start = ((), (), s32[]{:S(2)}) async-start(), calls=%async_computation.12 | async-start | bytes 10485760 | tf_op jit(solution)/shard_map/all_gather | solution.py:152
  166.5 467.9 %all-gather.18.cloned.1.call-start = ((), (), s32[]{:S(2)}) async-start(), calls=%async_computation.13 | async-start | bytes 10485760 | tf_op jit(solution)/shard_map/all_gather | solution.py:153
  167.2 556.4 %all-gather.20.cloned.1.call-start = ((), (), s32[]{:S(2)}) async-start(), calls=%async_computation.14 | async-start | bytes 10485760 | tf_op jit(solution)/shard_map/all_gather | solution.py:154
  168.0 293.7 %copy-start.56 = (f32[2048]{0:T(1024)S(1)}, f32[2048]{0:T(1024)}, u32[]{:S(2)}) copy-start(f32[2048]{0:T(1024)} %param.27) | copy-start | bytes 24580
  168.0 861.2 %all-reduce.12.cloned.1.call-start = ((), (), s32[]{:S(2)}) async-start(), calls=%async_computation.15 | async-start | bytes 16777216 | tf_op jit(solution)/shard_map/psum | solution.py:194
  456.9 5.8 copy-start
  738.2 295.1 %copy-start.55 = (f32[2048]{0:T(1024)S(1)}, f32[2048]{0:T(1024)}, u32[]{:S(2)}) copy-start(f32[2048]{0:T(1024)} %param.28) | copy-start | bytes 24580
  738.2 640.3 %all-reduce.14.cloned.1.call-start = ((), (), s32[]{:S(2)}) async-start(), calls=%async_computation.16 | async-start | bytes 16777216 | tf_op jit(solution)/shard_map/psum | solution.py:223
  1042.5 19.7 copy-start.34
  1062.2 12.7 copy-start.79
  1088.5 290.0 %copy-start.57 = (f32[2048]{0:T(1024)S(1)}, f32[2048]{0:T(1024)}, u32[]{:S(2)}) copy-start(f32[2048]{0:T(1024)} %param.27) | copy-start | bytes 24580
  1088.5 290.0 %copy-start.63 = (f32[1024]{0:T(1024)S(1)}, f32[1024]{0:T(1024)}, u32[]{:S(2)}) copy-start(f32[1024]{0:T(1024)} %copy-done.62) | copy-start | bytes 12292
  1088.6 466.7 %reduce-scatter.12.cloned.1.call-start = ((), (), s32[]{:S(2)}) async-start(), calls=%async_computation.20 | async-start | bytes 2621440 | tf_op jit(solution)/shard_map/reduce_scatter | solution.py:267
  1378.5 10.6 copy-start.3
  1378.5 10.6 copy-start.14
  1389.2 13.4 copy-start.52
  1389.2 13.4 copy-start.54
  1408.1 12.4 slice-start
  1413.1 7.4 slice-start.1
  1413.1 7.4 copy-start.30
  1413.2 7.4 copy-start.72
  1433.6 121.6 %reduce-scatter.10.cloned.1.call-start = ((), (), s32[]{:S(2)}) async-start(), calls=%async_computation.19 | async-start | bytes 2621440 | tf_op jit(solution)/shard_map/reduce_scatter | solution.py:264
  1439.4 7.2 copy-start.20
  1443.9 6.8 copy-start.21
  1486.4 72.1 %reduce-scatter.14.cloned.1.call-start = ((), (), s32[]{:S(2)}) async-start(), calls=%async_computation.21 | async-start | bytes 2621440 | tf_op jit(solution)/shard_map/reduce_scatter | solution.py:270
  1492.7 103.8 %reduce-scatter.8.cloned.1.call-start = ((), (), s32[]{:S(2)}) async-start(), calls=%async_computation.18 | async-start | bytes 2621440 | tf_op jit(solution)/shard_map/reduce_scatter | solution.py:261
  1499.6 186.2 %reduce-scatter.20.cloned.1.call-start = ((), (), s32[]{:S(2)}) async-start(), calls=%async_computation.24 | async-start | bytes 10485760 | tf_op jit(solution)/shard_map/reduce_scatter | solution.py:279
  1514.1 261.5 %reduce-scatter.16.cloned.1.call-start = ((), (), s32[]{:S(2)}) async-start(), calls=%async_computation.22 | async-start | bytes 10485760 | tf_op jit(solution)/shard_map/reduce_scatter | solution.py:273
  1528.2 336.7 %reduce-scatter.18.cloned.1.call-start = ((), (), s32[]{:S(2)}) async-start(), calls=%async_computation.23 | async-start | bytes 10485760 | tf_op jit(solution)/shard_map/reduce_scatter | solution.py:276
  1543.0 479.7 %all-reduce.16.cloned.1.call-start = ((), (), s32[]{:S(2)}) async-start(), calls=%async_computation.17 | async-start | bytes 8388608 | tf_op jit(solution)/shard_map/psum | solution.py:256
  1555.2 509.2 %all-reduce.18.cloned.1.call-start = ((), (), s32[]{:S(2)}) async-start(), calls=%async_computation.25 | async-start | bytes 16777216 | tf_op jit(solution)/shard_map/psum | solution.py:284
  2071.2 6.1 copy-start.47
  (53 other events, 164.5 us)
Sparse Core Ops, SparseCore 0:
  9.8 37.8 all-gather.11
  49.6 35.1 all-gather.9
  86.7 35.1 all-gather.7
  123.6 35.0 all-gather.13
  166.0 290.8 all-reduce.9
  458.6 86.4 all-gather.15
  546.9 87.4 all-gather.17
  636.2 87.3 all-gather.19
  738.3 290.8 all-reduce.11
  1088.7 289.7 all-reduce.13
  1433.7 34.1 reduce-scatter.11
  1486.5 33.7 reduce-scatter.9
  1523.2 35.1 reduce-scatter.13
  1561.3 35.1 reduce-scatter.7
  1599.4 86.3 reduce-scatter.19
  1689.3 86.3 reduce-scatter.15
  1778.5 86.3 reduce-scatter.17
  1867.7 154.9 all-reduce.15
  2026.0 38.3 all-reduce.17
where the time goes:
time: 2090 us
  waiting for transfers between devices  1650 us (79%)
  matrix products  236 us (11%)
  other arithmetic  103 us (5%)
  blocking collectives  49.6 us (2%)
  local copies, waits for them, and re-layouts  34.5 us (2%)
    psum x1, waiting for transfers between devices, shards(): down_raw = lax.psum(plain_dot(mixed_act, full_down), 'col')  291 us
    psum x1, waiting for transfers between devices, shards(): attn_raw = lax.psum(plain_dot(attended_flat, full_out), 'col')  289 us
    psum x1, waiting for transfers between devices, shards(): grad_hidden = grad_y + lax.psum(mlp_part, 'col')  288 us
    psum x1, waiting for transfers between devices, shards(): lax.psum(input_part.astype(jnp.bfloat16), 'col').astype(jnp.float32)  129 us
    reduce_scatter x1, waiting for transfers between devices, shards(): lax.psum_scatter(grad_w_gate.astype(jnp.bfloat16), 'row', scatter_dimensi...  89.8 us
    reduce_scatter x1, waiting for transfers between devices, shards(): lax.psum_scatter(grad_w_down.astype(jnp.bfloat16), 'row', scatter_dimensi...  89.3 us
    reduce_scatter x1, waiting for transfers between devices, shards(): lax.psum_scatter(grad_w_up.astype(jnp.bfloat16), 'row', scatter_dimension...  89.3 us
    all_gather x1, waiting for transfers between devices, shards(): lax.all_gather(w_gate, 'row', axis=0, tiled=True)  77.5 us
  transfers between devices with their start and end apart: 19, of which 16 were waited for; matrix products, arithmetic and copies ran while one was open for 10% of the time, Pallas kernels for 0%

commit v1 on v0

--- a/solution.py
+++ b/solution.py
@@ -181,7 +181,7 @@
     seg_view = segment_ids.reshape(seq_count, LEN)
     attended, log_total = lax.map(attend_forward, (query_rot, key_rot, value_heads, seg_view))
     attended_flat = attended.reshape(tokens_here, local_width)
-    attn_raw = lax.psum(plain_dot(attended_flat, full_out), "col")
+    attn_raw = jnp.sum(lax.all_gather(plain_dot(attended_flat, full_out), "col"), axis=0)
     attn_scale = lax.rsqrt(jnp.mean(attn_raw * attn_raw, axis=1, keepdims=True) + EPS)
     attn_unit = attn_raw * attn_scale
     hidden = block_input.astype(jnp.float32) + attn_unit * attn_gain

time: 2090 us -> 2360 us (1.13)
  waiting for transfers between devices: 1650 us -> 1900 us
    all_gather x0 -> x1, waiting for transfers between devices: none -> 559 us  [shards(): lax.all_gather(plain_dot(attended_flat, full_out), 'col')]
    psum x1 -> x0, waiting for transfers between devices: 289 us -> none  [shards(): attn_raw = lax.psum(plain_dot(attended_flat, full_out), 'col')]
where the time goes in v1:
time: 2360 us
  waiting for transfers between devices  1900 us (81%)
  matrix products  237 us (10%)
  other arithmetic  119 us (5%)
  blocking collectives  49.6 us (2%)
  local copies, waits for them, and re-layouts  34.6 us (1%)
    all_gather x1, waiting for transfers between devices, shards(): lax.all_gather(plain_dot(attended_flat, full_out), 'col')  559 us
    psum x1, waiting for transfers between devices, shards(): down_raw = lax.psum(plain_dot(mixed_act, full_down), 'col')  291 us
    psum x1, waiting for transfers between devices, shards(): grad_hidden = grad_y + lax.psum(mlp_part, 'col')  288 us
    psum x1, waiting for transfers between devices, shards(): lax.psum(input_part.astype(jnp.bfloat16), 'col').astype(jnp.float32)  129 us
    reduce_scatter x1, waiting for transfers between devices, shards(): lax.psum_scatter(grad_w_gate.astype(jnp.bfloat16), 'row', scatter_dimensi...  89.8 us
    reduce_scatter x1, waiting for transfers between devices, shards(): lax.psum_scatter(grad_w_down.astype(jnp.bfloat16), 'row', scatter_dimensi...  89.3 us
    reduce_scatter x1, waiting for transfers between devices, shards(): lax.psum_scatter(grad_w_up.astype(jnp.bfloat16), 'row', scatter_dimension...  89.2 us
    all_gather x1, waiting for transfers between devices, shards(): lax.all_gather(w_up, 'row', axis=0, tiled=True)  74.8 us
  transfers between devices with their start and end apart: 19, of which 16 were waited for; matrix products, arithmetic and copies ran while one was open for 10% of the time, Pallas kernels for 0%

profile of v1, /device:TPU:0, one launch (start us, length us, event | category | flops | bytes accessed | tf_op | source)
XLA Modules:
  0.0 2355.3 jit_solution(7983721926833220822)
XLA Ops:
  15.1 32.7 %all-gather.14.cloned.1.call-done = bf16[2048,512]{1,0:T(8,128)(2,1)} async-done(((bf16[512,512]{1,0:T(8,128)(2,1)}), bf16[2048,512]{1,0:T(8,128)(2,1)}) %all-gather.14.cloned.1.call-update) | async-done | bytes 2097168 | tf_op jit(solution)/shard_map/all_gather | solution.py:149
  47.8 6.6 multiply_reduce_fusion.7
  54.4 30.5 %all-gather.12.cloned.1.call-done = bf16[2048,512]{1,0:T(8,128)(2,1)} async-done(((bf16[512,512]{1,0:T(8,128)(2,1)}), bf16[2048,512]{1,0:T(8,128)(2,1)}) %all-gather.12.cloned.1.call-update) | async-done | bytes 2097168 | tf_op jit(solution)/shard_map/all_gather | solution.py:148
  84.8 5.2 multiply_reduce_fusion.8
  90.1 12.1 all-reduce.2
  123.6 4.7 exponential_reduce_fusion
  128.4 5.7 convolution_convert_fusion.8
  141.4 17.3 all-gather.16.cloned.1.call-done
  158.6 7.3 fusion.41
  168.1 559.4 %all-gather.24.cloned.1.call-done = f32[4096,2048]{1,0:T(8,128)} async-done(((f32[1024,2048]{1,0:T(8,128)}), f32[4096,2048]{1,0:T(8,128)}) %all-gather.24.cloned.1.call-update) | async-done | bytes 33554448 | tf_op jit(solution)/shard_map/all_gather | solution.py:184
  727.5 17.4 reduce_sum.151
  750.6 4.6 fusion.9
  755.2 59.7 %all-gather.18.cloned.1.call-done = bf16[2048,2048]{1,0:T(8,128)(2,1)} async-done(((bf16[512,2048]{1,0:T(8,128)(2,1)}), bf16[2048,2048]{1,0:T(8,128)(2,1)}) %all-gather.18.cloned.1.call-update) | async-done | bytes 8388624 | tf_op jit(solution)/shard_map/all_gather | solution.py:152
  814.9 14.6 fusion.42
  829.4 74.8 %all-gather.20.cloned.1.call-done = bf16[2048,2048]{1,0:T(8,128)(2,1)} async-done(((bf16[512,2048]{1,0:T(8,128)(2,1)}), bf16[2048,2048]{1,0:T(8,128)(2,1)}) %all-gather.20.cloned.1.call-update) | async-done | bytes 8388624 | tf_op jit(solution)/shard_map/all_gather | solution.py:153
  904.2 17.0 multiply_convert_fusion.5
  921.2 72.2 %all-gather.22.cloned.1.call-done = bf16[2048,2048]{1,0:T(8,128)(2,1)} async-done(((bf16[2048,512]{1,0:T(8,128)(2,1)}), bf16[2048,2048]{1,0:T(8,128)(2,1)}) %all-gather.22.cloned.1.call-update) | async-done | bytes 8388624 | tf_op jit(solution)/shard_map/all_gather | solution.py:154
  993.4 14.5 fusion.43
  1008.2 290.7 %all-reduce.9.cloned.1.call-done = f32[1024,2048]{1,0:T(8,128)} async-done(((f32[1024,2048]{1,0:T(8,128)}), f32[1024,2048]{1,0:T(8,128)}) %all-reduce.9.cloned.1.call-update) | async-done | bytes 8388624 | tf_op jit(solution)/shard_map/psum | solution.py:194
  1299.0 4.1 multiply_reduce_fusion.2
  1304.7 5.2 fusion.5
  1312.1 19.8 multiply_convert_fusion.3
  1331.9 12.7 fusion.44
  1344.7 13.6 convolution_add_fusion
  1360.4 287.9 %all-reduce.11.cloned.1.call-done = f32[1024,2048]{1,0:T(8,128)} async-done(((f32[1024,2048]{1,0:T(8,128)}), f32[1024,2048]{1,0:T(8,128)}) %all-reduce.11.cloned.1.call-update) | async-done | bytes 8388624 | tf_op jit(solution)/shard_map/psum | solution.py:223
  1648.3 10.5 multiply_reduce_fusion
  1658.8 13.4 multiply_convert_fusion.2
  1672.2 5.3 fusion.18
  1677.7 5.0 fusion.33
  1682.8 7.4 multiply_convert_fusion.1
  1690.2 5.1 multiply_convert_fusion
  1709.1 4.5 convolution_bitcast_fusion
  1734.4 4.3 multiply_reduce_fusion.4
  1739.4 9.6 all-reduce.1
  1756.2 6.2 convolution_convert_fusion.3
  1769.4 14.4 convolution_convert_fusion
  1783.9 14.1 convolution_convert_fusion.2
  1798.0 14.7 convolution_convert_fusion.1
  1819.2 5.7 add_convert_fusion
  1828.2 38.0 %reduce-scatter.8.cloned.1.call-done = bf16[512,512]{0,1:T(8,128)(2,1)} async-done(((bf16[2048,512]{0,1:T(8,128)(2,1)}), bf16[512,512]{0,1:T(8,128)(2,1)}) %reduce-scatter.8.cloned.1.call-update) | async-done | bytes 524304 | tf_op jit(solution)/shard_map/reduce_scatter | solution.py:261
  1866.3 89.3 %reduce-scatter.20.cloned.1.call-done = bf16[2048,512]{1,0:T(8,128)(2,1)} async-done(((bf16[2048,2048]{1,0:T(8,128)(2,1)}), bf16[2048,512]{1,0:T(8,128)(2,1)}) %reduce-scatter.20.cloned.1.call-update) | async-done | bytes 2097168 | tf_op jit(solution)/shard_map/reduce_scatter | solution.py:279
  1955.5 89.8 %reduce-scatter.16.cloned.1.call-done = bf16[512,2048]{1,0:T(8,128)(2,1)} async-done(((bf16[2048,2048]{1,0:T(8,128)(2,1)}), bf16[512,2048]{1,0:T(8,128)(2,1)}) %reduce-scatter.16.cloned.1.call-update) | async-done | bytes 2097168 | tf_op jit(solution)/shard_map/reduce_scatter | solution.py:273
  2045.4 89.2 %reduce-scatter.18.cloned.1.call-done = bf16[512,2048]{1,0:T(8,128)(2,1)} async-done(((bf16[2048,2048]{1,0:T(8,128)(2,1)}), bf16[512,2048]{1,0:T(8,128)(2,1)}) %reduce-scatter.18.cloned.1.call-update) | async-done | bytes 2097168 | tf_op jit(solution)/shard_map/reduce_scatter | solution.py:276
  2135.3 27.9 %all-reduce = (f32[512]{0:T(512)}, f32[512]{0:T(512)}, f32[2048]{0:T(1024)}, f32[2048]{0:T(1024)}) all-reduce(f32[512]{0:T(512)S(1)} %get-tuple-element.86, f32[512]{0:T(512)S(1)} %get-tuple-element.84, f32[2048]{0:T(1024)S(1)} %copy-done.64, f32[2048]{0:T(1024)S(1)} %copy-done.65), channel_id=1, replica_groups=mesh['dp'=2,'row'=4,'col'=4] {'dp','row'}, use_global_device_ids=true, to_apply=%region_36.37 | all-reduce | flops 5120 | bytes 40960 | tf_op jit(solution)/shard_map/psum | solution.py:292
  2163.2 129.2 %all-reduce.13.cloned.1.call-done = bf16[1024,2048]{1,0:T(8,128)(2,1)} async-done(((bf16[1024,2048]{1,0:T(8,128)(2,1)}), bf16[1024,2048]{1,0:T(8,128)(2,1)}) %all-reduce.13.cloned.1.call-update) | async-done | bytes 4194320 | tf_op jit(solution)/shard_map/psum | solution.py:256
  2292.4 12.0 convert_add_fusion.1
  2304.5 29.7 %all-reduce.15.cloned.1.call-done = (bf16[512,512]{0,1:T(8,128)(2,1)}, bf16[512,512]{0,1:T(8,128)(2,1)}, bf16[512,512]{0,1:T(8,128)(2,1)}, bf16[512,512]{1,0:T(8...) async-done(((bf16[512,512]{0,1:T(8,128)(2,1)}, bf16[512,512]{0,1:T(8,128)(2,1)}, bf16[512,512]{0,1:T(8,128)(2,1)}, ...) | async-done | bytes 8388624 | tf_op jit(solution)/shard_map/psum | solution.py:284
  2334.1 4.3 convert_element_type.217
  (268 shorter events, 119.6 us)
Async XLA Ops:
  7.2 5.9 copy-start.70
  7.2 40.6 %all-gather.14.cloned.1.call-start = ((), (), s32[]{:S(2)}) async-start(), calls=%async_computation.9 | async-start | bytes 2621440 | tf_op jit(solution)/shard_map/all_gather | solution.py:149
  7.9 76.9 %all-gather.12.cloned.1.call-start = ((), (), s32[]{:S(2)}) async-start(), calls=%async_computation.8 | async-start | bytes 2621440 | tf_op jit(solution)/shard_map/all_gather | solution.py:148
  8.7 119.8 %all-gather.10.cloned.1.call-start = ((), (), s32[]{:S(2)}) async-start(), calls=%async_computation.7 | async-start | bytes 2621440 | tf_op jit(solution)/shard_map/all_gather | solution.py:150
  9.4 149.2 %all-gather.16.cloned.1.call-start = ((), (), s32[]{:S(2)}) async-start(), calls=%async_computation.10 | async-start | bytes 2621440 | tf_op jit(solution)/shard_map/all_gather | solution.py:151
  10.0 717.5 %all-gather.24.cloned.1.call-start = ((), (), s32[]{:S(2)}) async-start(), calls=%async_computation.24 | async-start | bytes 41943040 | tf_op jit(solution)/shard_map/all_gather | solution.py:184
  12.8 103.1 %copy-start.22 = (f32[1024,128]{1,0:T(8,128)}, f32[1024,128]{1,0:T(8,128)S(1)}, u32[]{:S(2)}) copy-start(f32[1024,128]{1,0:T(8,128)S(1)} %pad_maximum_fusion.2) | copy-start | bytes 1572868
  13.1 102.9 %copy-start.27 = (f32[1024,128]{1,0:T(8,128)}, f32[1024,128]{1,0:T(8,128)S(1)}, u32[]{:S(2)}) copy-start(f32[1024,128]{1,0:T(8,128)S(1)} %pad_maximum_fusion.3) | copy-start | bytes 1572868
  54.3 47.9 %copy-start.68 = (f32[512]{0:T(512)S(1)}, f32[512]{0:T(512)}, u32[]{:S(2)}) copy-start(f32[512]{0:T(512)} %param.25) | copy-start | bytes 6148
  90.1 13.7 copy-start.9
  122.2 6.1 copy-start.5
  128.4 5.8 copy-start.73
  128.4 8.8 copy-start.71
  128.4 5.8 copy-start.32
  128.4 5.9 copy-start.8
  141.3 24.6 %copy-start.46 = (bf16[1024,4,128]{0,2,1:T(8,128)(2,1)}, bf16[1024,4,128]{0,2,1:T(8,128)(2,1)S(1)}, u32[]{:S(2)}) copy-start(bf16[1024,4,128]{0,2,1:T(8,128)(2,1)S(1)} %pad_maximum_fusion.1) | copy-start | bytes 3145732
  165.9 648.9 %all-gather.18.cloned.1.call-start = ((), (), s32[]{:S(2)}) async-start(), calls=%async_computation.11 | async-start | bytes 10485760 | tf_op jit(solution)/shard_map/all_gather | solution.py:152
  166.5 737.7 %all-gather.20.cloned.1.call-start = ((), (), s32[]{:S(2)}) async-start(), calls=%async_computation.12 | async-start | bytes 10485760 | tf_op jit(solution)/shard_map/all_gather | solution.py:153
  167.3 826.2 %all-gather.22.cloned.1.call-start = ((), (), s32[]{:S(2)}) async-start(), calls=%async_computation.13 | async-start | bytes 10485760 | tf_op jit(solution)/shard_map/all_gather | solution.py:154
  168.0 1130.9 %all-reduce.9.cloned.1.call-start = ((), (), s32[]{:S(2)}) async-start(), calls=%async_computation.14 | async-start | bytes 16777216 | tf_op jit(solution)/shard_map/psum | solution.py:194
  744.8 5.8 copy-start
  744.8 5.8 copy-start.56
  1008.0 295.1 %copy-start.55 = (f32[2048]{0:T(1024)S(1)}, f32[2048]{0:T(1024)}, u32[]{:S(2)}) copy-start(f32[2048]{0:T(1024)} %param.28) | copy-start | bytes 24580
  1008.0 640.3 %all-reduce.11.cloned.1.call-start = ((), (), s32[]{:S(2)}) async-start(), calls=%async_computation.15 | async-start | bytes 16777216 | tf_op jit(solution)/shard_map/psum | solution.py:223
  1312.1 19.8 copy-start.34
  1331.9 12.7 copy-start.79
  1358.3 290.0 %copy-start.57 = (f32[2048]{0:T(1024)S(1)}, f32[2048]{0:T(1024)}, u32[]{:S(2)}) copy-start(f32[2048]{0:T(1024)} %param.27) | copy-start | bytes 24580
  1358.3 290.0 %copy-start.63 = (f32[1024]{0:T(1024)S(1)}, f32[1024]{0:T(1024)}, u32[]{:S(2)}) copy-start(f32[1024]{0:T(1024)} %copy-done.62) | copy-start | bytes 12292
  1358.3 466.7 %reduce-scatter.12.cloned.1.call-start = ((), (), s32[]{:S(2)}) async-start(), calls=%async_computation.19 | async-start | bytes 2621440 | tf_op jit(solution)/shard_map/reduce_scatter | solution.py:267
  1648.3 10.5 copy-start.3
  1648.3 10.5 copy-start.14
  1658.8 13.4 copy-start.52
  1658.8 13.4 copy-start.54
  1677.7 12.5 slice-start
  1682.7 7.5 slice-start.1
  1682.7 7.5 copy-start.30
  1682.8 7.4 copy-start.72
  1703.3 121.7 %reduce-scatter.10.cloned.1.call-start = ((), (), s32[]{:S(2)}) async-start(), calls=%async_computation.18 | async-start | bytes 2621440 | tf_op jit(solution)/shard_map/reduce_scatter | solution.py:264
  1709.1 7.2 copy-start.20
  1713.6 6.8 copy-start.21
  1756.2 72.1 %reduce-scatter.14.cloned.1.call-start = ((), (), s32[]{:S(2)}) async-start(), calls=%async_computation.20 | async-start | bytes 2621440 | tf_op jit(solution)/shard_map/reduce_scatter | solution.py:270
  1762.4 103.8 %reduce-scatter.8.cloned.1.call-start = ((), (), s32[]{:S(2)}) async-start(), calls=%async_computation.17 | async-start | bytes 2621440 | tf_op jit(solution)/shard_map/reduce_scatter | solution.py:261
  1769.3 186.2 %reduce-scatter.20.cloned.1.call-start = ((), (), s32[]{:S(2)}) async-start(), calls=%async_computation.23 | async-start | bytes 10485760 | tf_op jit(solution)/shard_map/reduce_scatter | solution.py:279
  1783.9 261.5 %reduce-scatter.16.cloned.1.call-start = ((), (), s32[]{:S(2)}) async-start(), calls=%async_computation.21 | async-start | bytes 10485760 | tf_op jit(solution)/shard_map/reduce_scatter | solution.py:273
  1798.0 336.6 %reduce-scatter.18.cloned.1.call-start = ((), (), s32[]{:S(2)}) async-start(), calls=%async_computation.22 | async-start | bytes 10485760 | tf_op jit(solution)/shard_map/reduce_scatter | solution.py:276
  1812.8 479.7 %all-reduce.13.cloned.1.call-start = ((), (), s32[]{:S(2)}) async-start(), calls=%async_computation.16 | async-start | bytes 8388608 | tf_op jit(solution)/shard_map/psum | solution.py:256
  1825.0 509.2 %all-reduce.15.cloned.1.call-start = ((), (), s32[]{:S(2)}) async-start(), calls=%async_computation.25 | async-start | bytes 16777216 | tf_op jit(solution)/shard_map/psum | solution.py:284
  2341.0 6.1 copy-start.47
  (53 other events, 164.7 us)
Sparse Core Ops, SparseCore 0:
  9.8 37.8 all-gather.13
  49.6 35.1 all-gather.11
  86.7 35.1 all-gather.9
  123.6 35.0 all-gather.15
  166.1 561.3 all-gather.23
  729.2 85.6 all-gather.17
  816.7 87.4 all-gather.19
  906.1 87.3 all-gather.21
  1008.1 290.8 all-reduce.8
  1358.4 289.7 all-reduce.10
  1703.4 34.1 reduce-scatter.11
  1756.3 33.7 reduce-scatter.9
  1793.0 35.1 reduce-scatter.13
  1831.0 35.1 reduce-scatter.7
  1869.2 86.3 reduce-scatter.19
  1959.0 86.3 reduce-scatter.15
  2048.3 86.2 reduce-scatter.17
  2137.4 154.9 all-reduce.12
  2295.8 38.3 all-reduce.14
